TPU v7x, 32 devices: a whole 2x2x4 slice. The times are simulated.
32 devices in a mesh: row: 8 (over y, x, core), col: 4 (over z).
Axes of the slice: x: 2, y: 2, z: 4, core: 2. Of those that a mesh axis runs over, the one named last changes fastest.
Arguments:
- final_amp: bfloat16 [8, 32, 128, 440], P('row', 'col'), may hold values from -0.19921875 to 0.19921875
- initial_amp: bfloat16 [4, 32, 128, 440], P('col', 'row'), may hold values from -0.19921875 to 0.19921875
- pair_final: int32 [8, 4, 128], P('row', 'col'), may hold values from 0 to 31
- pair_initial: int32 [8, 4, 128], P('row', 'col'), may hold values from 0 to 31
- map_final: int32 [8, 32, 440], P('row', 'col'), may hold values from 0 to 439, each once within a row
- map_initial: int32 [4, 32, 440], P('col', 'row'), may hold values from 0 to 439, each once within a row
- counts: int32 [8, 4], P('row', 'col'), may hold values from 16 to 128, as said below
Outputs:
- density: float32 [440, 440], replicated
Inputs may be any that keep to these rules, and one draw needn't show every extreme that they name: `counts`: slots at or past a cell's count are ignored. Exactly one cell of every draw has 128 live slots.
All inputs are finite; a program needn't handle non-finite values.
Results may differ from a plain program's by a relative error of at most 0.0003.
Values may be sent and summed in bfloat16 or wider, within the bound.
A program may use at most 64 MiB of HBM per device.

v0:
```python
import jax
import jax.numpy as jnp
from jax import lax
from jax.sharding import PartitionSpec as P

GROUP = 32


def permute_columns(blocks, orbital_map):
    return jnp.take(blocks, orbital_map, axis=1)


def shards(final_amp, initial_amp, pair_final, pair_initial, map_final, map_initial, counts):
    own_final = jax.vmap(permute_columns)(final_amp[0], map_final[0])[None]
    own_initial = jax.vmap(permute_columns)(initial_amp[0], map_initial[0])[None]
    row_seg = lax.all_gather(own_final, "col", axis=1, tiled=True)[0]
    column_seg = lax.all_gather(own_initial, "row", axis=1, tiled=True)[0]
    slots_final = pair_final[0, 0]
    slots_initial = pair_initial[0, 0]
    live_count = counts[0, 0]
    orbitals = final_amp.shape[3]
    group_size = GROUP

    def advance(index, summed):
        first_slot = index * group_size
        which_final = lax.dynamic_slice_in_dim(slots_final, first_slot, group_size)
        which_initial = lax.dynamic_slice_in_dim(slots_initial, first_slot, group_size)
        live_mask = first_slot + jnp.arange(group_size, dtype=jnp.int32) < live_count
        left = jnp.take(row_seg, which_final, axis=0)
        right = jnp.take(column_seg, which_initial, axis=0)
        left = jnp.where(live_mask[:, None, None], left, jnp.zeros_like(left))
        product = lax.dot_general(
            left.reshape(-1, orbitals),
            right.reshape(-1, orbitals),
            (((0,), (0,)), ((), ())),
            preferred_element_type=jnp.float32,
        )
        return summed + product

    turns = (live_count + group_size - 1) // group_size
    partial_density = lax.fori_loop(0, turns, advance, jnp.zeros((orbitals, orbitals), jnp.float32))
    band = lax.psum_scatter(partial_density, "col", scatter_dimension=0, tiled=True)
    band = lax.psum(band, "row")
    density = lax.all_gather(band, "col", axis=0, tiled=True)
    return density


def solution(mesh):
    placed = (
        P("row", "col", None, None),
        P("col", "row", None, None),
        P("row", "col", None),
        P("row", "col", None),
        P("row", "col", None),
        P("col", "row", None),
        P("row", "col"),
    )
    return jax.shard_map(shards, mesh=mesh, in_specs=placed, out_specs=P(), check_vma=False)
```

profile of v0, /device:TPU:0, one launch (start us, length us, event | category | flops | bytes accessed | tf_op | source)
XLA Modules:
  0.0 321.1 jit_solution(12124861493017973160)
XLA Ops:
  6.5 0.8 fusion.18
  7.3 0.7 compare_and_fusion.2
  8.2 30.8 %gather_fusion.2 = bf16[3520,128]{1,0:T(8,128)(2,1)S(1)} fusion(bf16[8,128,440]{1,2,0:T(8,128)(2,1)S(1)} %bitcast.44, s32[3520]{0:T(1024)S(1)} %reshape.110), kind=kCustom, calls=%fused_computation.2 | custom fusion | bytes 1830400 | tf_op jit(solution)/shard_map/vmap(jit(_take))/gather | solution.py:10
  39.0 1.4 broadcast_select_fusion
  40.5 15.7 %gather_fusion.3 = bf16[1760,128]{1,0:T(8,128)(2,1)S(1)} fusion(bf16[4,128,440]{1,2,0:T(8,128)(2,1)S(1)} %bitcast.45, s32[1760]{0:T(1024)S(1)} %reshape.116), kind=kCustom, calls=%fused_computation.3 | custom fusion | bytes 915200 | tf_op jit(solution)/shard_map/vmap(jit(_take))/gather | solution.py:10
  56.3 1.1 broadcast_select_fusion.1
  58.2 56.1 %all-gather.4.cloned.1.call-done = bf16[1,32,128,440]{2,3,0,1:T(8,128)(2,1)} async-done(((bf16[1,8,128,440]{2,3,0,1:T(8,128)(2,1)}), bf16[1,32,128,440]{2,3,0,1:T(8,128)(2,1)}) %all-gather.4.cloned.1.call-update) | async-done | bytes 3604496 | tf_op jit(solution)/shard_map/all_gather | solution.py:16
  114.3 6.4 %copy.18 = bf16[32,128,440]{2,1,0:T(8,128)(2,1)} copy(bf16[32,128,440]{1,2,0:T(8,128)(2,1)} %bitcast.47) | data formatting | bytes 7208960 | tf_op jit(solution)/shard_map/while | solution.py:41
  120.7 28.2 %all-gather.6.cloned.1.call-done = bf16[1,32,128,440]{2,3,0,1:T(8,128)(2,1)} async-done(((bf16[1,4,128,440]{2,3,0,1:T(8,128)(2,1)}), bf16[1,32,128,440]{2,3,0,1:T(8,128)(2,1)}) %all-gather.6.cloned.1.call-update) | async-done | bytes 3604496 | tf_op jit(solution)/shard_map/all_gather | solution.py:17
  148.9 6.5 %copy.19 = bf16[32,128,440]{2,1,0:T(8,128)(2,1)} copy(bf16[32,128,440]{1,2,0:T(8,128)(2,1)} %bitcast.48) | data formatting | bytes 7208960 | tf_op jit(solution)/shard_map/while | solution.py:41
  155.3 0.1 broadcast_in_dim.43
  155.5 33.5 %while.10 = (s32[]{:T(128)}, f32[440,440]{1,0:T(8,128)S(1)}, s32[]{:T(128)}, s32[]{:T(128)}, s32[128]{0:T(128)S(1)}, /*index=5*/bf16[32,128,440]{2,1,0:T(8,128)(...) while((s32[]{:T(128)}, f32[440,440]{1,0:T(8,128)S(1)}, ...), condition=%wide.region_1.3_spmd, body=%wide.region_0.0_spmd.sunk | while | flops 1591574016 | bytes 23185264 | solution.py:41
  155.5 0.1 compare_and_fusion.5
  155.6 5.0 %gather_fusion = bf16[32,128,440]{2,1,0:T(8,128)(2,1)} fusion(bf16[32,128,440]{2,1,0:T(8,128)(2,1)} %get-tuple-element.169, s32[1024]{0:T(1024)S(1)} %pad_clamp_fusion.4), kind=kCustom, calls=%fused_computation.1.clone.clone.1 | custom fusion | bytes 7209088 | tf_op jit(solution)/shard_map/while/body/jit(_take)/gather | solution.py:30
  160.6 4.9 %gather_fusion.1 = bf16[32,128,440]{2,1,0:T(8,128)(2,1)} fusion(bf16[32,128,440]{2,1,0:T(8,128)(2,1)} %get-tuple-element.167, s32[1024]{0:T(1024)S(1)} %pad_clamp_fusion.5), kind=kCustom, calls=%fused_computation.clone.clone.1 | custom fusion | bytes 7209088 | tf_op jit(solution)/shard_map/while/body/jit(_take)/gather | solution.py:29
  165.5 0.7 add_compare_fusion.2
  166.1 6.1 %fusion.25 = f32[440,440]{1,0:T(8,128)S(1)} fusion(f32[440,440]{1,0:T(8,128)S(1)} %get-tuple-element.151, bf16[32,128,440]{2,1,0:T(8,128)(2,1)} %gather_fusion, pred[32]{0:T(512)(128)(4,1)S(1)} %get-tuple-element.135, bf16[32,128,440]{2,1,0:T(8,128)(2,1)} %gather_fusion.1, pred[32]{0:T(512)(128)(4,1)S(1)} %get-tuple-element.137, ...), kind=kOutput, calls=%fused_computation.13.clone.1 | convolution fusion | flops 1591571456 | bytes 8757856 | tf_op jit(solution)/shard_map/while/body/dot_general | solution.py:32
  172.3 5.0 %gather_fusion = bf16[32,128,440]{2,1,0:T(8,128)(2,1)} fusion(bf16[32,128,440]{2,1,0:T(8,128)(2,1)} %get-tuple-element.169, s32[1024]{0:T(1024)S(1)} %pad_clamp_fusion.4), kind=kCustom, calls=%fused_computation.1.clone.clone.1 | custom fusion | bytes 7209088 | tf_op jit(solution)/shard_map/while/body/jit(_take)/gather | solution.py:30
  177.3 4.9 %gather_fusion.1 = bf16[32,128,440]{2,1,0:T(8,128)(2,1)} fusion(bf16[32,128,440]{2,1,0:T(8,128)(2,1)} %get-tuple-element.167, s32[1024]{0:T(1024)S(1)} %pad_clamp_fusion.5), kind=kCustom, calls=%fused_computation.clone.clone.1 | custom fusion | bytes 7209088 | tf_op jit(solution)/shard_map/while/body/jit(_take)/gather | solution.py:29
  182.2 0.7 add_compare_fusion.2
  182.9 6.1 %fusion.25 = f32[440,440]{1,0:T(8,128)S(1)} fusion(f32[440,440]{1,0:T(8,128)S(1)} %get-tuple-element.151, bf16[32,128,440]{2,1,0:T(8,128)(2,1)} %gather_fusion, pred[32]{0:T(512)(128)(4,1)S(1)} %get-tuple-element.135, bf16[32,128,440]{2,1,0:T(8,128)(2,1)} %gather_fusion.1, pred[32]{0:T(512)(128)(4,1)S(1)} %get-tuple-element.137, ...), kind=kOutput, calls=%fused_computation.13.clone.1 | convolution fusion | flops 1591571456 | bytes 8757856 | tf_op jit(solution)/shard_map/while/body/dot_general | solution.py:32
  188.9 22.8 %fusion = f32[112,440]{1,0:T(8,128)S(1)} fusion(f32[440,440]{1,0:T(8,128)S(1)} %get-tuple-element.49), kind=kCustom, calls=%all-reduce-scatter | all-reduce-scatter fusion | flops 197121 | bytes 972032
  211.7 2.1 collective-permute-start
  213.9 0.6 dynamic-slice.4
  215.1 0.2 collective-permute-done
  215.3 0.2 concatenate.6
  215.6 0.7 constant_dynamic-slice_fusion
  216.3 74.9 %all-reduce.4.cloned.1.call-done = f32[110,440]{1,0:T(8,128)} async-done(((f32[110,440]{1,0:T(8,128)}), f32[110,440]{1,0:T(8,128)}) %all-reduce.4.cloned.1.call-update) | async-done | bytes 193616 | tf_op jit(solution)/shard_map/psum | solution.py:43
  291.2 1.1 copy.20
  292.3 20.9 %all-gather = f32[4,110,440]{1,2,0:T(8,128)S(1)} all-gather(f32[1,110,440]{1,2,0:T(8,128)S(1)} %copy.20), channel_id=1, replica_groups=mesh['row'=8,'col'=4] {'col'}, dimensions={0}, use_global_device_ids=true | all-gather | bytes 968000 | tf_op jit(solution)/shard_map/all_gather | solution.py:44
  313.2 0.4 copy.21
  313.6 1.0 reshape.125
  (28 shorter events, 0.5 us)
Async XLA Ops:
  6.5 1.6 copy-start
  6.5 107.7 %all-gather.4.cloned.1.call-start = ((), (), s32[]{:S(2)}) async-start(), calls=%async_computation | async-start | bytes 4505600 | tf_op jit(solution)/shard_map/all_gather | solution.py:16
  8.2 32.3 %copy-start.2 = (s32[1,4,440]{2,1,0:T(4,128)S(1)}, s32[1,4,440]{2,1,0:T(4,128)}, u32[]{:S(2)}) copy-start(s32[1,4,440]{2,1,0:T(4,128)} %param.16) | copy-start | bytes 21124
  8.2 32.4 %copy-start.1 = (bf16[1,4,128,440]{2,3,1,0:T(8,128)(2,1)S(1)}, bf16[1,4,128,440]{2,3,1,0:T(8,128)(2,1)}, u32[]{:S(2)}) copy-start(bf16[1,4,128,440]{2,3,1,0:T(8,128)(2,1)} %param.12) | copy-start | bytes 1351684
  40.4 108.5 %all-gather.6.cloned.1.call-start = ((), (), s32[]{:S(2)}) async-start(), calls=%async_computation.1 | async-start | bytes 4055040 | tf_op jit(solution)/shard_map/all_gather | solution.py:17
  57.4 233.8 %all-reduce.4.cloned.1.call-start = ((), (), s32[]{:S(2)}) async-start(), calls=%async_computation.2 | async-start | bytes 458752 | tf_op jit(solution)/shard_map/psum | solution.py:43
  148.9 6.6 %copy-start.3 = (s32[1,1,128]{2,1,0:T(1,128)S(1)}, s32[1,1,128]{2,1,0:T(1,128)}, u32[]{:S(2)}) copy-start(s32[1,1,128]{2,1,0:T(1,128)} %param.13) | copy-start | bytes 1540
  148.9 6.6 %copy-start.4 = (s32[1,1,128]{2,1,0:T(1,128)S(1)}, s32[1,1,128]{2,1,0:T(1,128)}, u32[]{:S(2)}) copy-start(s32[1,1,128]{2,1,0:T(1,128)} %param.14) | copy-start | bytes 1540
  155.5 58.4 %copy-start.5 = (u32[32]{0:T(128)S(1)}, u32[32]{0:T(128)}, u32[]{:S(2)}) copy-start(u32[32]{0:T(128)} %constant.104) | copy-start | bytes 388
  211.7 3.6 %collective-permute-start = (f32[6,440]{1,0:T(8,128)S(1)}, f32[6,440]{1,0:T(8,128)S(1)}, u32[]{:S(2)}, u32[]{:S(2)}) collective-permute-start(f32[6,440]{1,0:T(8,128)S(1)} %slice.8), channel_id=1, source_target_pairs={{0,1},{1,2},{2,3},{4,5},{5,6},{6,7},{8,9},{9,10},{10,11},{12,13},{... | collective-permute-start | bytes 31688
Sparse Core Ops, SparseCore 0:
  40.5 73.7 all-gather.3
  116.2 32.6 all-gather.5
  216.4 74.7 all-reduce.3
where the time goes:
time: 322 us; the launch traced here: 321 us
  waiting for transfers between devices  159 us (49%)
  local copies, waits for them, and re-layouts  83.4 us (26%)
  blocking collectives  43.7 us (14%)
  between operations  14.6 us (5%)
  matrix products  12.1 us (4%)
  other arithmetic  5.57 us (2%)
    psum x1, waiting for transfers between devices, shards(): band = lax.psum(band, 'row')  74.9 us
    all_gather x1, waiting for transfers between devices, shards(): row_seg = lax.all_gather(own_final, 'col', axis=1, tiled=True)[0]  56.1 us
    gather x4, local copies, waits for them, and re-layouts, permute_columns(): return jnp.take(blocks, orbital_map, axis=1)  46.6 us
    all_gather x1, waiting for transfers between devices, shards(): column_seg = lax.all_gather(own_initial, 'row', axis=1, tiled=True)[0]  28.2 us
    unnamed x1, blocking collectives  22.8 us
    all_gather x1, blocking collectives, shards(): density = lax.all_gather(band, 'col', axis=0, tiled=True)  20.9 us
    while x2, local copies, waits for them, and re-layouts, shards(): lax.fori_loop(0, turns, advance, jnp.zeros((orbitals, orbitals), jnp.floa...  12.9 us
    dot_general x2, matrix products, advance(): lax.dot_general(left.reshape(-1, orbitals), right.reshape(-1, orbitals),...  12.1 us
  transfers between devices with their start and end apart: 4, of which 4 were waited for; matrix products, arithmetic and copies ran while one was open for 7% of the time, Pallas kernels for 0%

commit v1 on v0

--- a/solution.py
+++ b/solution.py
@@ -4,6 +4,12 @@
 from jax.sharding import PartitionSpec as P
 
 GROUP = 32
+
+
+def limits_handle(q_in, dimension_no):
+    finding = list(q_in.shape[1:])
+    finding[dimension_no] *= q_in.shape[0]
+    return jnp.moveaxis(q_in, 0, dimension_no).reshape(finding)
 
 
 def permute_columns(blocks, orbital_map):
@@ -13,7 +19,18 @@
 def shards(final_amp, initial_amp, pair_final, pair_initial, map_final, map_initial, counts):
     own_final = jax.vmap(permute_columns)(final_amp[0], map_final[0])[None]
     own_initial = jax.vmap(permute_columns)(initial_amp[0], map_initial[0])[None]
-    row_seg = lax.all_gather(own_final, "col", axis=1, tiled=True)[0]
+
+    def serve_chains(local, which_axis, join_dim):
+        size_here = lax.axis_size(which_axis)
+        pile = [local]
+        all_blocks = list(map(lambda tick: (tick, (tick + 1) % size_here), range(size_here)))
+        while len(pile) < size_here:
+            pile.append(lax.ppermute(pile[-1], which_axis, all_blocks))
+        block_out = lax.axis_index(which_axis)
+        pile = jnp.stack(pile)[(block_out - jnp.arange(size_here)) % size_here]
+        return limits_handle(pile, join_dim)
+
+    row_seg = serve_chains(own_final, which_axis="col", join_dim=1)[0]
     column_seg = lax.all_gather(own_initial, "row", axis=1, tiled=True)[0]
     slots_final = pair_final[0, 0]
     slots_initial = pair_initial[0, 0]

time: 322 us -> 308 us (0.957)
  waiting for transfers between devices: 159 us -> 137 us
  local copies, waits for them, and re-layouts: 83.4 us -> 89.1 us
  blocking collectives: 43.7 us -> 39.4 us
  starting transfers between devices: 2.22 us -> 6.2 us
    ppermute x0 -> x3, waiting for transfers between devices: none -> 66.1 us  [serve_chains(): pile.append(lax.ppermute(pile[-1], which_axis, all_blocks))]
    all_gather x1 -> x0, waiting for transfers between devices: 56.1 us -> none  [shards(): row_seg = lax.all_gather(own_final, 'col', axis=1, tiled=True)[0]]
    all_gather x1, waiting for transfers between devices: 28.2 us -> 0.01 us  [shards(): column_seg = lax.all_gather(own_initial, 'row', axis=1, tiled=True)[0]]
    gather x0 -> x2, local copies, waits for them, and re-layouts: none -> 11 us  [serve_chains(): pile = jnp.stack(pile)[(block_out - jnp.arange(size_here)) % size_here]]
    while x2 -> x1, local copies, waits for them, and re-layouts: 12.9 us -> 6.46 us  [shards(): lax.fori_loop(0, turns, advance, jnp.zeros((orbitals, orbitals), jnp.floa...]
    psum x1, waiting for transfers between devices: 74.9 us -> 70.4 us  [shards(): band = lax.psum(band, 'row')]
    unnamed x1, blocking collectives: 22.8 us -> 18.5 us
  transfers between devices with their start and end apart: 4 -> 6, of which waited for: 4 -> 5; matrix products, arithmetic and copies ran while one was open for 7% -> 15% of each run, Pallas kernels for 0% -> 0%
where the time goes in v1:
time: 308 us; the launch traced here: 307 us
  waiting for transfers between devices  137 us (44%)
  local copies, waits for them, and re-layouts  89.1 us (29%)
  blocking collectives  39.4 us (13%)
  between operations  14.9 us (5%)
  matrix products  12.1 us (4%)
  other arithmetic  8.56 us (3%)
  starting transfers between devices  6.2 us (2%)
    psum x1, waiting for transfers between devices, shards(): band = lax.psum(band, 'row')  70.4 us
    ppermute x3, waiting for transfers between devices, serve_chains(): pile.append(lax.ppermute(pile[-1], which_axis, all_blocks))  66.1 us
    gather x4, local copies, waits for them, and re-layouts, permute_columns(): return jnp.take(blocks, orbital_map, axis=1)  47.7 us
    all_gather x1, blocking collectives, shards(): density = lax.all_gather(band, 'col', axis=0, tiled=True)  20.9 us
    unnamed x1, blocking collectives  18.5 us
    dot_general x2, matrix products, advance(): lax.dot_general(left.reshape(-1, orbitals), right.reshape(-1, orbitals),...  12.1 us
    gather x2, local copies, waits for them, and re-layouts, serve_chains(): pile = jnp.stack(pile)[(block_out - jnp.arange(size_here)) % size_here]  11 us
    gather x2, local copies, waits for them, and re-layouts, advance(): right = jnp.take(column_seg, which_initial, axis=0)  9.93 us
  transfers between devices with their start and end apart: 6, of which 5 were waited for; matrix products, arithmetic and copies ran while one was open for 15% of the time, Pallas kernels for 0%

profile of v1, /device:TPU:0, one launch (start us, length us, event | category | flops | bytes accessed | tf_op | source)
XLA Modules:
  0.0 307.1 jit_solution(8209272381759934323)
XLA Ops:
  6.5 0.8 fusion.21
  7.3 0.7 compare_and_fusion.3
  8.1 16.7 %gather_fusion.4 = bf16[1760,128]{1,0:T(8,128)(2,1)S(1)} fusion(bf16[4,128,440]{1,2,0:T(8,128)(2,1)} %bitcast.55, s32[1760]{0:T(1024)S(1)} %reshape.182), kind=kCustom, calls=%fused_computation.4 | custom fusion | bytes 915200 | tf_op jit(solution)/shard_map/vmap(jit(_take))/gather | solution.py:16
  24.9 1.1 broadcast_select_fusion.2
  26.1 30.8 %gather_fusion.3 = bf16[3520,128]{1,0:T(8,128)(2,1)S(1)} fusion(bf16[8,128,440]{1,2,0:T(8,128)(2,1)S(1)} %bitcast.53, s32[3520]{0:T(1024)S(1)} %reshape.176), kind=kCustom, calls=%fused_computation.3 | custom fusion | bytes 1830400 | tf_op jit(solution)/shard_map/vmap(jit(_take))/gather | solution.py:16
  56.9 0.7 broadcast_select_fusion
  57.6 3.1 %collective-permute-start = (bf16[1,8,128,440]{2,3,1,0:T(8,128)(2,1)S(1)}, bf16[1,8,128,440]{2,3,1,0:T(8,128)(2,1)S(1)}, u32[]{:S(2)}, u32[]{:S(2)}) collective-permute-start(bf16[1,8,128,440]{2,3,1,0:T(8,128)(2,1)S(1)} %broadcast_select_fusion), channel_id=1, source_target_pairs={{0,1},{1,2},{2,3},{3,0},{4,5},{5,6},{6,7},{7,4},{8,9},{9,10},{10,1... | collective-permute-start | bytes 2703368 | tf_op jit(solution)/shard_map/ppermute | solution.py:28
  60.7 22.0 %collective-permute-done = bf16[1,8,128,440]{2,3,1,0:T(8,128)(2,1)S(1)} collective-permute-done((bf16[1,8,128,440]{2,3,1,0:T(8,128)(2,1)S(1)}, bf16[1,8,128,440]{2,3,1,0:T(8,128)(2,1)S(1)}, u32[]{:S(2)}, u32[]{:S(2)}) %collective-permute-start) | collective-permute-done | bytes 901152 | tf_op jit(solution)/shard_map/ppermute | solution.py:28
  82.7 23.1 %collective-permute-done.1 = bf16[1,8,128,440]{2,3,1,0:T(8,128)(2,1)} collective-permute-done((bf16[1,8,128,440]{2,3,1,0:T(8,128)(2,1)S(1)}, bf16[1,8,128,440]{2,3,1,0:T(8,128)(2,1)}, u32[]{:S(2)}, u32[]{:S(2)}) %collective-permute-start.1) | collective-permute-done | bytes 901152 | tf_op jit(solution)/shard_map/ppermute | solution.py:28
  106.5 0.7 broadcast_select_fusion.1
  107.1 21.1 %collective-permute-done.2 = bf16[1,8,128,440]{2,3,1,0:T(8,128)(2,1)} collective-permute-done((bf16[1,8,128,440]{2,3,1,0:T(8,128)(2,1)}, bf16[1,8,128,440]{2,3,1,0:T(8,128)(2,1)}, u32[]{:S(2)}, u32[]{:S(2)}) %collective-permute-start.2) | collective-permute-done | bytes 901152 | tf_op jit(solution)/shard_map/ppermute | solution.py:28
  128.2 3.2 %maximum_bitcast_fusion = bf16[4,8,128,440]{2,3,1,0:T(8,128)(2,1)} fusion(bf16[1,1,8,128,440]{3,4,2,1,0:T(8,128)(2,1)} %bitcast.13, bf16[1,1,8,128,440]{3,4,2,1,0:T(8,128)(2,1)} %bitcast.12, bf16[1,1,8,128,440]{3,4,2,1,0:T(8,128)(2,1)S(1)} %bitcast.60, bf16[1,1,8,128,440]{3,4,2,1,0:T(8,128)(2,1)S(1)} %broadcast_select_fusion.1), kind=kLoop, calls=%fused_computation.24 | loop fusion | flops 5406720 | bytes 7208960 | tf_op jit(solution)/shard_map/stack | solution.py:30
  131.4 4.8 %gather_fusion.2 = bf16[4,8,128,440]{2,3,1,0:T(8,128)(2,1)} fusion(bf16[4,8,128,440]{2,3,1,0:T(8,128)(2,1)} %maximum_bitcast_fusion, s32[1024]{0:T(1024)S(1)} %pad_clamp_fusion.2), kind=kCustom, calls=%fused_computation.2 | custom fusion | bytes 7208976 | tf_op jit(solution)/shard_map/gather | solution.py:30
  136.2 6.2 %copy.18 = bf16[4,8,128,440]{3,2,1,0:T(8,128)(2,1)} copy(bf16[4,8,128,440]{2,3,1,0:T(8,128)(2,1)} %gather_fusion.2) | data formatting | bytes 7208960 | tf_op jit(solution)/shard_map/gather | solution.py:30
  142.4 6.5 %copy.19 = bf16[32,128,440]{2,1,0:T(8,128)(2,1)} copy(bf16[32,128,440]{1,2,0:T(8,128)(2,1)} %bitcast.58) | data formatting | bytes 7208960 | tf_op jit(solution)/shard_map/while | solution.py:58
  149.0 33.5 %while.10 = (s32[]{:T(128)}, f32[440,440]{1,0:T(8,128)S(1)}, s32[]{:T(128)}, s32[]{:T(128)}, s32[128]{0:T(128)S(1)}, /*index=5*/bf16[32,128,440]{2,1,0:T(8,128)(...) while((s32[]{:T(128)}, f32[440,440]{1,0:T(8,128)S(1)}, ...), condition=%wide.region_1.3_spmd, body=%wide.region_0.0_spmd.sunk | while | flops 1591574016 | bytes 23185264 | solution.py:58
  149.1 4.9 %gather_fusion.1 = bf16[32,128,440]{2,1,0:T(8,128)(2,1)} fusion(bf16[32,128,440]{2,1,0:T(8,128)(2,1)} %get-tuple-element.167, s32[1024]{0:T(1024)S(1)} %pad_clamp_fusion.6), kind=kCustom, calls=%fused_computation.clone.clone.1 | custom fusion | bytes 7209088 | tf_op jit(solution)/shard_map/while/body/jit(_take)/gather | solution.py:46
  154.0 5.0 %gather_fusion = bf16[32,128,440]{2,1,0:T(8,128)(2,1)} fusion(bf16[32,128,440]{2,1,0:T(8,128)(2,1)} %get-tuple-element.169, s32[1024]{0:T(1024)S(1)} %pad_clamp_fusion.5), kind=kCustom, calls=%fused_computation.1.clone.clone.1 | custom fusion | bytes 7209088 | tf_op jit(solution)/shard_map/while/body/jit(_take)/gather | solution.py:47
  159.0 0.7 add_compare_fusion.2
  159.7 6.1 %fusion.27 = f32[440,440]{1,0:T(8,128)S(1)} fusion(f32[440,440]{1,0:T(8,128)S(1)} %get-tuple-element.151, bf16[32,128,440]{2,1,0:T(8,128)(2,1)} %gather_fusion, pred[32]{0:T(512)(128)(4,1)S(1)} %get-tuple-element.135, bf16[32,128,440]{2,1,0:T(8,128)(2,1)} %gather_fusion.1, pred[32]{0:T(512)(128)(4,1)S(1)} %get-tuple-element.137, ...), kind=kOutput, calls=%fused_computation.14.clone.1 | convolution fusion | flops 1591571456 | bytes 8757856 | tf_op jit(solution)/shard_map/while/body/dot_general | solution.py:49
  165.8 4.9 %gather_fusion.1 = bf16[32,128,440]{2,1,0:T(8,128)(2,1)} fusion(bf16[32,128,440]{2,1,0:T(8,128)(2,1)} %get-tuple-element.167, s32[1024]{0:T(1024)S(1)} %pad_clamp_fusion.6), kind=kCustom, calls=%fused_computation.clone.clone.1 | custom fusion | bytes 7209088 | tf_op jit(solution)/shard_map/while/body/jit(_take)/gather | solution.py:46
  170.8 5.0 %gather_fusion = bf16[32,128,440]{2,1,0:T(8,128)(2,1)} fusion(bf16[32,128,440]{2,1,0:T(8,128)(2,1)} %get-tuple-element.169, s32[1024]{0:T(1024)S(1)} %pad_clamp_fusion.5), kind=kCustom, calls=%fused_computation.1.clone.clone.1 | custom fusion | bytes 7209088 | tf_op jit(solution)/shard_map/while/body/jit(_take)/gather | solution.py:47
  175.7 0.7 add_compare_fusion.2
  176.4 6.1 %fusion.27 = f32[440,440]{1,0:T(8,128)S(1)} fusion(f32[440,440]{1,0:T(8,128)S(1)} %get-tuple-element.151, bf16[32,128,440]{2,1,0:T(8,128)(2,1)} %gather_fusion, pred[32]{0:T(512)(128)(4,1)S(1)} %get-tuple-element.135, bf16[32,128,440]{2,1,0:T(8,128)(2,1)} %gather_fusion.1, pred[32]{0:T(512)(128)(4,1)S(1)} %get-tuple-element.137, ...), kind=kOutput, calls=%fused_computation.14.clone.1 | convolution fusion | flops 1591571456 | bytes 8757856 | tf_op jit(solution)/shard_map/while/body/dot_general | solution.py:49
  182.5 18.5 %fusion = f32[112,440]{1,0:T(8,128)S(1)} fusion(f32[440,440]{1,0:T(8,128)S(1)} %get-tuple-element.49), kind=kCustom, calls=%all-reduce-scatter | all-reduce-scatter fusion | flops 197121 | bytes 972032
  201.0 3.0 collective-permute-start.3
  204.1 0.6 dynamic-slice.4
  205.8 0.7 constant_dynamic-slice_fusion
  206.5 70.4 %all-reduce.4.cloned.1.call-done = f32[110,440]{1,0:T(8,128)} async-done(((f32[110,440]{1,0:T(8,128)}), f32[110,440]{1,0:T(8,128)}) %all-reduce.4.cloned.1.call-update) | async-done | bytes 193616 | tf_op jit(solution)/shard_map/psum | solution.py:60
  276.9 1.1 copy.20
  278.0 20.9 %all-gather = f32[4,110,440]{1,2,0:T(8,128)S(1)} all-gather(f32[1,110,440]{1,2,0:T(8,128)S(1)} %copy.20), channel_id=1, replica_groups=mesh['row'=8,'col'=4] {'col'}, dimensions={0}, use_global_device_ids=true | all-gather | bytes 968000 | tf_op jit(solution)/shard_map/all_gather | solution.py:61
  299.3 1.0 reshape.192
  (34 shorter events, 1.4 us)
Async XLA Ops:
  6.5 19.6 %copy-start = (bf16[1,8,128,440]{2,3,1,0:T(8,128)(2,1)S(1)}, bf16[1,8,128,440]{2,3,1,0:T(8,128)(2,1)}, u32[]{:S(2)}) copy-start(bf16[1,8,128,440]{2,3,1,0:T(8,128)(2,1)} %param.11) | copy-start | bytes 2703364
  6.5 19.5 %copy-start.1 = (s32[1,8,440]{2,1,0:T(8,128)S(1)}, s32[1,8,440]{2,1,0:T(8,128)}, u32[]{:S(2)}) copy-start(s32[1,8,440]{2,1,0:T(8,128)} %param.15) | copy-start | bytes 42244
  6.5 135.8 %all-gather.3.cloned.1.call-start = ((), (), s32[]{:S(2)}) async-start(), calls=%async_computation | async-start | bytes 4055040 | tf_op jit(solution)/shard_map/all_gather | solution.py:34
  26.0 250.9 %all-reduce.4.cloned.1.call-start = ((), (), s32[]{:S(2)}) async-start(), calls=%async_computation.1 | async-start | bytes 458752 | tf_op jit(solution)/shard_map/psum | solution.py:60
  57.6 25.1 %collective-permute-start = (bf16[1,8,128,440]{2,3,1,0:T(8,128)(2,1)S(1)}, bf16[1,8,128,440]{2,3,1,0:T(8,128)(2,1)S(1)}, u32[]{:S(2)}, u32[]{:S(2)}) collective-permute-start(bf16[1,8,128,440]{2,3,1,0:T(8,128)(2,1)S(1)} %broadcast_select_fusion), channel_id=1, source_target_pairs={{0,1},{1,2},{2,3},{3,0},{4,5},{5,6},{6,7},{7,4},{8,9},{9,10},{10,1... | collective-permute-start | bytes 2703368 | tf_op jit(solution)/shard_map/ppermute | solution.py:28
  82.7 23.1 %collective-permute-start.1 = (bf16[1,8,128,440]{2,3,1,0:T(8,128)(2,1)S(1)}, bf16[1,8,128,440]{2,3,1,0:T(8,128)(2,1)}, u32[]{:S(2)}, u32[]{:S(2)}) collective-permute-start(bf16[1,8,128,440]{2,3,1,0:T(8,128)(2,1)S(1)} %collective-permute-done), channel_id=1, source_target_pairs={{0,1},{1,2},{2,3},{3,0},{4,5},{5,6},{6,7},{7,4},{8,9},{9,10},{10,1... | collective-permute-start | bytes 2703368 | tf_op jit(solution)/shard_map/ppermute | solution.py:28
  105.8 22.4 %collective-permute-start.2 = (bf16[1,8,128,440]{2,3,1,0:T(8,128)(2,1)}, bf16[1,8,128,440]{2,3,1,0:T(8,128)(2,1)}, u32[]{:S(2)}, u32[]{:S(2)}) collective-permute-start(bf16[1,8,128,440]{2,3,1,0:T(8,128)(2,1)} %collective-permute-done.1), channel_id=1, source_target_pairs={{0,1},{1,2},{2,3},{3,0},{4,5},{5,6},{6,7},{7,4},{8,9},{9,10},{10,1... | collective-permute-start | bytes 2703368 | tf_op jit(solution)/shard_map/ppermute | solution.py:28
  142.4 6.6 %copy-start.2 = (s32[1,1,128]{2,1,0:T(1,128)S(1)}, s32[1,1,128]{2,1,0:T(1,128)}, u32[]{:S(2)}) copy-start(s32[1,1,128]{2,1,0:T(1,128)} %param.13) | copy-start | bytes 1540
  142.4 6.6 %copy-start.3 = (s32[1,1,128]{2,1,0:T(1,128)S(1)}, s32[1,1,128]{2,1,0:T(1,128)}, u32[]{:S(2)}) copy-start(s32[1,1,128]{2,1,0:T(1,128)} %param.14) | copy-start | bytes 1540
  149.0 55.1 %copy-start.4 = (u32[32]{0:T(128)S(1)}, u32[32]{0:T(128)}, u32[]{:S(2)}) copy-start(u32[32]{0:T(128)} %constant.124) | copy-start | bytes 388
  201.0 4.5 %collective-permute-start.3 = (f32[6,440]{1,0:T(8,128)S(1)}, f32[6,440]{1,0:T(8,128)S(1)}, u32[]{:S(2)}, u32[]{:S(2)}) collective-permute-start(f32[6,440]{1,0:T(8,128)S(1)} %slice.10), channel_id=1, source_target_pairs={{0,1},{1,2},{2,3},{4,5},{5,6},{6,7},{8,9},{9,10},{10,11},{12,13},{... | collective-permute-start | bytes 31688
Sparse Core Ops, SparseCore 0:
  26.1 36.8 all-gather.2
  206.6 70.2 all-reduce.3
